TPU v7x, 128 devices: a whole 4x4x4 slice. The times are simulated.
128 devices in a mesh: req: 4 (over y), tp: 32 (over x, z, core).
Axes of the slice: x: 4, y: 4, z: 4, core: 2. Of those that a mesh axis runs over, the one named last changes fastest.
Arguments:
- hidden_states: bfloat16 [16, 4, 1024], P('req'), may hold values from -48 to 48
- lengths: int32 [16], P('req'), may hold values from 16 to 4096, as said below
- qkv_weight: bfloat16 [2048, 1024], P('tp'), may hold values from -1 to 1
- rotated_key_cache: bfloat16 [16, 4096, 512], P('req', 'tp'), may hold values from -1000 to 1000
- earlier_value_cache: bfloat16 [16, 4096, 512], P('req', 'tp'), may hold values from -16 to 16
- out_weight: bfloat16 [1024, 1024], P('tp'), may hold values from -0.1875 to 0.1875
- expert_ids: int32 [16, 4, 8], P('req'), may hold values from 0 to 31, all different within a row
- combine_weights: int32 [16, 4, 8], P('req'), may hold values from 4096 to 65535
- gate_up_weight: bfloat16 [32, 1024, 1024], P('tp'), may hold values from -0.1875 to 0.1875
- down_weight: bfloat16 [32, 512, 1024], P('tp'), may hold values from -0.25 to 0.25
Outputs:
- layer_output: bfloat16 [16, 4, 1024], P('req')
Inputs may be any that keep to these rules, and one draw needn't show every extreme that they name: `lengths`: cache length of each request; some request has exactly 4096. `expert_ids`: each token's 8 experts are distinct.
All inputs are finite; a program needn't handle non-finite values.
Results may differ from a plain program's by a relative error of at most 0.008.
Values may be sent and summed in bfloat16 or wider, within the bound.
A program may use at most 64 MiB of HBM per device.

v0:
```python
import jax
import jax.numpy as jnp
from jax import lax
from jax.sharding import PartitionSpec as P

QUERY_HEADS = 16
KEY_VALUE_HEADS = 8
HEAD_DIMENSION = 64
EPSILON = 1e-05
ROPE_BASE = 10000.0
NEGATIVE = -1e30


def merged(part, axis, combine):
    gathered = jax.tree.map(lambda a: lax.all_gather(a, axis), part)

    def take(source):
        return jax.tree.map(lambda a: lax.dynamic_index_in_dim(a, source, 0, False), gathered)

    return lax.fori_loop(
        1, lax.axis_size(axis), lambda source, state: combine(state, take(source)), take(0)
    )


def rms_rows(value_rows):
    return value_rows * lax.rsqrt(
        jnp.mean(value_rows * value_rows, axis=-1, keepdims=True) + EPSILON
    )


def apply_rotation(value_rows, position_index):
    half_width = value_rows.shape[-1] // 2
    rates = ROPE_BASE ** (-2.0 * jnp.arange(half_width, dtype=jnp.float32) / value_rows.shape[-1])
    angles = position_index[:, None, None] * rates
    cosine = jnp.cos(angles)
    sines = jnp.sin(angles)
    front_half = value_rows[..., :half_width]
    back_half = value_rows[..., half_width:]
    return jnp.concatenate(
        [front_half * cosine - back_half * sines, back_half * cosine + front_half * sines], axis=-1
    )


def join_parts(earlier, later):
    highest = jnp.maximum(earlier[0], later[0])
    scale_earlier = jnp.exp(earlier[0] - highest)
    scale_later = jnp.exp(later[0] - highest)
    weight_sum = earlier[1] * scale_earlier + later[1] * scale_later
    value_sum = earlier[2] * scale_earlier[..., None] + later[2] * scale_later[..., None]
    return (highest, weight_sum, value_sum)


def to_columns(value_rows, step_number, group_count):
    request_list, kv_heads, _, head_size = value_rows.shape
    return (
        value_rows.reshape(request_list, kv_heads, step_number, group_count, head_size)
        .transpose(0, 2, 1, 3, 4)
        .reshape(request_list * step_number, kv_heads * group_count * head_size)
    )


def expert_terms(normed, chosen, shares, gate_up_weight, down_weight, first_expert):
    ff_width = down_weight.shape[1]
    united_out = jnp.einsum(
        "nd,edf->enf", normed, gate_up_weight, preferred_element_type=jnp.float32
    )
    activation = (jax.nn.silu(united_out[..., :ff_width]) * united_out[..., ff_width:]).astype(
        jnp.bfloat16
    )
    outcome = jnp.einsum(
        "enf,efd->end", activation, down_weight, preferred_element_type=jnp.float32
    )
    owners = first_expert + jnp.arange(gate_up_weight.shape[0], dtype=jnp.int32)
    factors = jnp.sum(
        jnp.where(chosen[None, :, :] == owners[:, None, None], shares[None, :, :], 0.0), axis=-1
    )
    return jnp.sum(factors[:, :, None] * outcome, axis=0)


def per_device(
    hidden_states,
    lengths,
    qkv_weight,
    rotated_key_cache,
    earlier_value_cache,
    out_weight,
    expert_ids,
    combine_weights,
    gate_up_weight,
    down_weight,
):
    request_list, step_number, model_width = hidden_states.shape
    token_rows = request_list * step_number
    group_count = QUERY_HEADS // KEY_VALUE_HEADS
    query_total_width = QUERY_HEADS * HEAD_DIMENSION
    key_value_width = KEY_VALUE_HEADS * HEAD_DIMENSION
    score_scale = HEAD_DIMENSION ** (-0.5)
    inputs_flat = hidden_states.reshape(token_rows, model_width)
    normed = rms_rows(inputs_flat.astype(jnp.float32)).astype(jnp.bfloat16)
    projected_part = lax.dot_general(
        qkv_weight, normed, (((1,), (1,)), ((), ())), preferred_element_type=jnp.float32
    ).astype(jnp.bfloat16)
    projected_all = lax.all_gather(projected_part, "tp", axis=0, tiled=True)
    query_key_value_rows = projected_all.T
    position_index = (
        (lengths[:, None] + jnp.arange(step_number, dtype=jnp.int32)[None, :])
        .reshape(token_rows)
        .astype(jnp.float32)
    )
    query_rows = apply_rotation(
        query_key_value_rows[:, :query_total_width]
        .reshape(token_rows, QUERY_HEADS, HEAD_DIMENSION)
        .astype(jnp.float32),
        position_index,
    ).astype(jnp.bfloat16)
    fresh_keys = apply_rotation(
        query_key_value_rows[:, query_total_width : query_total_width + key_value_width]
        .reshape(token_rows, KEY_VALUE_HEADS, HEAD_DIMENSION)
        .astype(jnp.float32),
        position_index,
    ).astype(jnp.bfloat16)
    fresh_values = query_key_value_rows[:, query_total_width + key_value_width :].reshape(
        request_list, step_number, KEY_VALUE_HEADS, HEAD_DIMENSION
    )
    grouped_rows = (
        query_rows.reshape(request_list, step_number, KEY_VALUE_HEADS, group_count, HEAD_DIMENSION)
        .transpose(0, 2, 1, 3, 4)
        .reshape(request_list, KEY_VALUE_HEADS, step_number * group_count, HEAD_DIMENSION)
    )
    cache_extent = rotated_key_cache.shape[1]
    stored_keys = rotated_key_cache.reshape(
        request_list, cache_extent, KEY_VALUE_HEADS, HEAD_DIMENSION
    )
    stored_values = earlier_value_cache.reshape(
        request_list, cache_extent, KEY_VALUE_HEADS, HEAD_DIMENSION
    )
    scores = (
        jnp.einsum("bgqd,bcgd->bgqc", grouped_rows, stored_keys, preferred_element_type=jnp.float32)
        * score_scale
    )
    start_pos = lax.axis_index("tp") * cache_extent
    live_rows = (start_pos + jnp.arange(cache_extent, dtype=jnp.int32))[None, :] < lengths[:, None]
    live_mask = live_rows[:, None, None, :]
    masked = jnp.where(live_mask, scores, NEGATIVE)
    highest = jnp.max(masked, axis=-1)
    weights = jnp.where(live_mask, jnp.exp(masked - highest[..., None]), 0.0)
    weight_sum = jnp.sum(weights, axis=-1)
    value_sum = jnp.einsum(
        "bgqc,bcgd->bgqd",
        weights.astype(jnp.bfloat16),
        stored_values,
        preferred_element_type=jnp.float32,
    )
    feature_rows = out_weight.shape[0]
    column_begin = lax.axis_index("tp") * feature_rows
    top_score, total_all, sum_all = merged((highest, weight_sum, value_sum), "tp", join_parts)
    grouped_keys = fresh_keys.reshape(request_list, step_number, KEY_VALUE_HEADS, HEAD_DIMENSION)
    new_scores = (
        jnp.einsum(
            "bgqd,bsgd->bgqs", grouped_rows, grouped_keys, preferred_element_type=jnp.float32
        )
        * score_scale
    )
    query_step = jnp.arange(step_number * group_count, dtype=jnp.int32) // group_count
    causal = jnp.arange(step_number, dtype=jnp.int32)[None, :] <= query_step[:, None]
    new_masked = jnp.where(causal, new_scores, NEGATIVE)
    final_peak = jnp.maximum(top_score, jnp.max(new_masked, axis=-1))
    new_weights = jnp.where(causal, jnp.exp(new_masked - final_peak[..., None]), 0.0)
    carried = jnp.exp(top_score - final_peak)
    denominator = total_all * carried + jnp.sum(new_weights, axis=-1)
    new_part = jnp.einsum(
        "bgqs,bsgd->bgqd",
        new_weights.astype(jnp.bfloat16),
        fresh_values,
        preferred_element_type=jnp.float32,
    )
    numerator = sum_all * carried[..., None] + new_part
    attended = to_columns(numerator / denominator[..., None], step_number, group_count).astype(
        jnp.bfloat16
    )
    attended_part = lax.dynamic_slice_in_dim(attended, column_begin, feature_rows, 1)
    first_expert = lax.axis_index("tp") * gate_up_weight.shape[0]
    chosen = expert_ids.reshape(token_rows, -1)
    shares = combine_weights.reshape(token_rows, -1).astype(jnp.float32) / 65536.0
    head_terms = jnp.dot(attended_part, out_weight, preferred_element_type=jnp.float32)
    projected_rows = lax.psum(head_terms, "tp")
    residual = inputs_flat.astype(jnp.float32) + projected_rows
    normed_second = rms_rows(residual).astype(jnp.bfloat16)
    mixture = lax.psum(
        expert_terms(
            normed_second, chosen, shares, gate_up_weight, down_weight, first_expert
        ).astype(jnp.bfloat16),
        "tp",
    ).astype(jnp.float32)
    final_result = (residual + mixture).astype(jnp.bfloat16)
    return final_result.reshape(request_list, step_number, model_width)


def solution(mesh):
    in_specs = (
        P("req", None, None),
        P("req"),
        P("tp", None),
        P("req", "tp", None),
        P("req", "tp", None),
        P("tp", None),
        P("req", None, None),
        P("req", None, None),
        P("tp", None, None),
        P("tp", None, None),
    )
    out_specs = P("req", None, None)
    return jax.shard_map(
        per_device, mesh=mesh, in_specs=in_specs, out_specs=out_specs, check_vma=False
    )
```

profile of v0, /device:TPU:0, one launch (start us, length us, event | category | flops | bytes accessed | tf_op | source)
XLA Modules:
  0.0 358.4 jit_solution(16797033778908578031)
XLA Ops:
  10.0 1.1 fusion.13
  11.1 26.0 %all-gather.3 = bf16[32,64,16]{1,2,0:T(8,128)(2,1)S(1)} all-gather(bf16[1,64,16]{1,2,0:T(8,128)(2,1)S(1)} %fusion.13), channel_id=1, replica_groups=mesh['req'=4,'tp'=32] {'tp'}, dimensions={0}, use_global_device_ids=true | all-gather | bytes 67584 | tf_op jit(solution)/shard_map/all_gather | solution.py:103
  38.2 1.3 copy.24
  39.8 1.1 fusion.17
  42.7 24.2 %all-gather.1 = f32[128,8,8]{2,1,0:T(8,128)S(1)} all-gather(f32[4,8,8]{2,1,0:T(8,128)S(1)} %fusion.16), channel_id=3, replica_groups=mesh['req'=4,'tp'=32] {'tp'}, dimensions={0}, use_global_device_ids=true | all-gather | bytes 33792 | tf_op jit(solution)/shard_map/all_gather | solution.py:15
  67.0 22.6 %all-gather = f32[128,8,8]{2,1,0:T(8,128)S(1)} all-gather(f32[4,8,8]{2,1,0:T(8,128)S(1)} %get-tuple-element.216), channel_id=2, replica_groups=mesh['req'=4,'tp'=32] {'tp'}, dimensions={0}, use_global_device_ids=true | all-gather | bytes 33792 | tf_op jit(solution)/shard_map/all_gather | solution.py:15
  91.5 34.9 %while.19 = (s32[]{:T(128)}, f32[4,8,8]{2,1,0:T(8,128)S(1)}, f32[4,8,8]{2,1,0:T(8,128)S(1)}, f32[4,8,8,64]{3,2,1,0:T(8,128)S(1)}, f32[32,4,8,8]{3,2,1,0:T(8,128)...) while((s32[]{:T(128)}, f32[4,8,8]{2,1,0:T(8,128)S(1)}, ...), condition=%wide.region_4.5_spmd, body=%wide.region_3.4_spmd.sunk | while | flops 50693 | bytes 206991 | solution.py:20
  91.6 1.1 fusion.57
  92.7 1.1 fusion.57
  93.8 1.1 fusion.57
  95.0 1.1 fusion.57
  96.1 1.1 fusion.57
  97.2 1.1 fusion.57
  99.5 1.1 fusion.57
  100.6 1.1 fusion.57
  101.7 1.1 fusion.57
  102.9 1.1 fusion.57
  104.0 1.1 fusion.57
  105.1 1.1 fusion.57
  106.2 1.1 fusion.57
  107.4 1.1 fusion.57
  109.6 1.1 fusion.57
  130.0 93.8 %all-reduce.2.cloned.1.call-done = f32[16,1024]{1,0:T(8,128)} async-done(((f32[16,1024]{1,0:T(8,128)}), f32[16,1024]{1,0:T(8,128)}) %all-reduce.2.cloned.1.call-update) | async-done | bytes 65552 | tf_op jit(solution)/shard_map/psum | solution.py:186
  225.5 125.4 %psum.15 = bf16[16,1024]{1,0:T(8,128)(2,1)S(1)} all-reduce(bf16[16,1024]{1,0:T(8,128)(2,1)S(1)} %fusion.12), channel_id=1, replica_groups=mesh['req'=4,'tp'=32] {'tp'}, use_global_device_ids=true, to_apply=%region_10.11 | all-reduce | flops 16384 | bytes 65536 | tf_op jit(solution)/shard_map/psum | solution.py:189
  (109 shorter events, 32.2 us)
Async XLA Ops:
  6.5 218.2 %copy-start = (bf16[1,1024,1024]{2,1,0:T(8,128)(2,1)S(1)}, bf16[1,1024,1024]{2,1,0:T(8,128)(2,1)}, u32[]{:S(2)}) copy-start(bf16[1,1024,1024]{2,1,0:T(8,128)(2,1)} %param.20) | copy-start | bytes 6291460
  6.5 31.4 %copy-start.2 = (bf16[4,128,512]{2,1,0:T(8,128)(2,1)S(1)}, bf16[4,128,512]{2,1,0:T(8,128)(2,1)}, u32[]{:S(2)}) copy-start(bf16[4,128,512]{2,1,0:T(8,128)(2,1)} %param.15) | copy-start | bytes 1572868
  6.5 84.1 %all-gather.6.cloned.1.call-start = ((), (), s32[]{:S(2)}) async-start(), calls=%async_computation.1 | async-start | bytes 4325376 | tf_op jit(solution)/shard_map/all_gather | solution.py:15
  40.9 182.9 %all-reduce.2.cloned.1.call-start = ((), (), s32[]{:S(2)}) async-start(), calls=%async_computation | async-start | bytes 131072 | tf_op jit(solution)/shard_map/psum | solution.py:186
  89.5 1.0 copy-start.4
  91.5 36.8 %copy-start.3 = (bf16[32,1024]{1,0:T(8,128)(2,1)S(1)}, bf16[32,1024]{1,0:T(8,128)(2,1)}, u32[]{:S(2)}) copy-start(bf16[32,1024]{1,0:T(8,128)(2,1)} %param.17) | copy-start | bytes 196612
  126.5 98.7 %copy-start.1 = (bf16[1,512,1024]{2,1,0:T(8,128)(2,1)S(1)}, bf16[1,512,1024]{2,1,0:T(8,128)(2,1)}, u32[]{:S(2)}) copy-start(bf16[1,512,1024]{2,1,0:T(8,128)(2,1)} %param.21) | copy-start | bytes 3145732
Sparse Core Ops, SparseCore 0:
  41.1 45.7 all-gather.5
  129.3 94.4 all-reduce.1
where the time goes:
time: 359 us; the launch traced here: 358 us
  blocking collectives  198 us (55%)
  waiting for transfers between devices  93.8 us (26%)
  other arithmetic  39.8 us (11%)
  between operations  13.6 us (4%)
  local copies, waits for them, and re-layouts  6.09 us (2%)
  matrix products  5.89 us (2%)
    psum x1, blocking collectives, per_device(): lax.psum(expert_terms(normed_second, chosen, shares, gate_up_weight, down...  125 us
    psum x1, waiting for transfers between devices, per_device(): projected_rows = lax.psum(head_terms, 'tp')  93.8 us
    all_gather x2, blocking collectives, merged(): gathered = jax.tree.map(lambda a: lax.all_gather(a, axis), part)  46.8 us
    add x31, other arithmetic, join_parts(): earlier[2] * scale_earlier[..., None] + later[2] * scale_later[..., None]  33.3 us
    all_gather x1, blocking collectives, per_device(): projected_all = lax.all_gather(projected_part, 'tp', axis=0, tiled=True)  26 us
  transfers between devices with their start and end apart: 2, of which 1 were waited for; matrix products, arithmetic and copies ran while one was open for 1% of the time, Pallas kernels for 0%

commit v1 on v0

--- a/solution.py
+++ b/solution.py
@@ -183,7 +183,7 @@
     chosen = expert_ids.reshape(token_rows, -1)
     shares = combine_weights.reshape(token_rows, -1).astype(jnp.float32) / 65536.0
     head_terms = jnp.dot(attended_part, out_weight, preferred_element_type=jnp.float32)
-    projected_rows = lax.psum(head_terms, "tp")
+    projected_rows = jnp.sum(lax.all_gather(head_terms, "tp"), axis=0)
     residual = inputs_flat.astype(jnp.float32) + projected_rows
     normed_second = rms_rows(residual).astype(jnp.bfloat16)
     mixture = lax.psum(

time: 359 us -> 311 us (0.87)
  waiting for transfers between devices: 93.8 us -> 42.4 us
    psum x1 -> x0, waiting for transfers between devices: 93.8 us -> none  [per_device(): projected_rows = lax.psum(head_terms, 'tp')]
    all_gather x0 -> x1, waiting for transfers between devices: none -> 42.3 us  [per_device(): projected_rows = jnp.sum(lax.all_gather(head_terms, 'tp'), axis=0)]
  transfers between devices with their start and end apart: 2 -> 2, of which waited for: 1 -> 1; matrix products, arithmetic and copies ran while one was open for 1% -> 2% of each run, Pallas kernels for 0% -> 0%
where the time goes in v1:
time: 311 us; the launch traced here: 310 us
  blocking collectives  199 us (64%)
  waiting for transfers between devices  42.4 us (14%)
  other arithmetic  41.4 us (13%)
  between operations  13.6 us (4%)
  matrix products  6.52 us (2%)
  local copies, waits for them, and re-layouts  6.15 us (2%)
    psum x1, blocking collectives, per_device(): lax.psum(expert_terms(normed_second, chosen, shares, gate_up_weight, down...  126 us
    all_gather x2, blocking collectives, merged(): gathered = jax.tree.map(lambda a: lax.all_gather(a, axis), part)  47 us
    all_gather x1, waiting for transfers between devices, per_device(): projected_rows = jnp.sum(lax.all_gather(head_terms, 'tp'), axis=0)  42.3 us
    add x31, other arithmetic, join_parts(): earlier[2] * scale_earlier[..., None] + later[2] * scale_later[..., None]  33.3 us
    all_gather x1, blocking collectives, per_device(): projected_all = lax.all_gather(projected_part, 'tp', axis=0, tiled=True)  26 us
  transfers between devices with their start and end apart: 2, of which 1 were waited for; matrix products, arithmetic and copies ran while one was open for 2% of the time, Pallas kernels for 0%

profile of v1, /device:TPU:0, one launch (start us, length us, event | category | flops | bytes accessed | tf_op | source)
XLA Modules:
  0.0 310.3 jit_solution(518869353712301778)
XLA Ops:
  10.0 1.1 fusion.13
  11.1 26.0 %all-gather.4 = bf16[32,64,16]{1,2,0:T(8,128)(2,1)S(1)} all-gather(bf16[1,64,16]{1,2,0:T(8,128)(2,1)S(1)} %fusion.13), channel_id=1, replica_groups=mesh['req'=4,'tp'=32] {'tp'}, dimensions={0}, use_global_device_ids=true | all-gather | bytes 67584 | tf_op jit(solution)/shard_map/all_gather | solution.py:103
  38.2 1.3 copy.24
  39.8 1.1 fusion.17
  43.3 24.2 %all-gather.1 = f32[128,8,8]{2,1,0:T(8,128)S(1)} all-gather(f32[4,8,8]{2,1,0:T(8,128)S(1)} %fusion.16), channel_id=3, replica_groups=mesh['req'=4,'tp'=32] {'tp'}, dimensions={0}, use_global_device_ids=true | all-gather | bytes 33792 | tf_op jit(solution)/shard_map/all_gather | solution.py:15
  67.5 22.8 %all-gather = f32[128,8,8]{2,1,0:T(8,128)S(1)} all-gather(f32[4,8,8]{2,1,0:T(8,128)S(1)} %get-tuple-element.214), channel_id=2, replica_groups=mesh['req'=4,'tp'=32] {'tp'}, dimensions={0}, use_global_device_ids=true | all-gather | bytes 33792 | tf_op jit(solution)/shard_map/all_gather | solution.py:15
  90.3 1.6 fusion.46
  92.9 34.9 %while.19 = (s32[]{:T(128)}, f32[4,8,8]{2,1,0:T(8,128)S(1)}, f32[4,8,8]{2,1,0:T(8,128)S(1)}, f32[4,8,8,64]{3,2,1,0:T(8,128)S(1)}, f32[32,4,8,8]{3,2,1,0:T(8,128)...) while((s32[]{:T(128)}, f32[4,8,8]{2,1,0:T(8,128)S(1)}, ...), condition=%wide.region_4.5_spmd, body=%wide.region_3.4_spmd.sunk | while | flops 50693 | bytes 206991 | solution.py:20
  93.0 1.1 fusion.57
  94.1 1.1 fusion.57
  95.2 1.1 fusion.57
  96.3 1.1 fusion.57
  97.5 1.1 fusion.57
  98.6 1.1 fusion.57
  99.7 1.1 fusion.57
  100.8 1.1 fusion.57
  102.0 1.1 fusion.57
  104.2 1.1 fusion.57
  105.3 1.1 fusion.57
  106.5 1.1 fusion.57
  107.6 1.1 fusion.57
  131.5 42.3 %all-gather.10.cloned.1.call-done = f32[512,1024]{1,0:T(8,128)} async-done(((f32[16,1024]{1,0:T(8,128)}), f32[512,1024]{1,0:T(8,128)}) %all-gather.10.cloned.1.call-update) | async-done | bytes 2097168 | tf_op jit(solution)/shard_map/all_gather | solution.py:186
  173.8 1.8 reduce_sum.63
  176.5 126.3 %psum.7 = bf16[16,1024]{1,0:T(8,128)(2,1)S(1)} all-reduce(bf16[16,1024]{1,0:T(8,128)(2,1)S(1)} %fusion.12), channel_id=1, replica_groups=mesh['req'=4,'tp'=32] {'tp'}, use_global_device_ids=true, to_apply=%region_10.11 | all-reduce | flops 16384 | bytes 65536 | tf_op jit(solution)/shard_map/psum | solution.py:189
  (119 shorter events, 33.2 us)
Async XLA Ops:
  6.5 169.3 %copy-start = (bf16[1,1024,1024]{2,1,0:T(8,128)(2,1)S(1)}, bf16[1,1024,1024]{2,1,0:T(8,128)(2,1)}, u32[]{:S(2)}) copy-start(bf16[1,1024,1024]{2,1,0:T(8,128)(2,1)} %param.20) | copy-start | bytes 6291460
  6.5 31.4 %copy-start.3 = (bf16[4,128,512]{2,1,0:T(8,128)(2,1)S(1)}, bf16[4,128,512]{2,1,0:T(8,128)(2,1)}, u32[]{:S(2)}) copy-start(bf16[4,128,512]{2,1,0:T(8,128)(2,1)} %param.15) | copy-start | bytes 1572868
  6.5 85.4 %all-gather.8.cloned.1.call-start = ((), (), s32[]{:S(2)}) async-start(), calls=%async_computation | async-start | bytes 4325376 | tf_op jit(solution)/shard_map/all_gather | solution.py:15
  9.8 30.0 %copy-start.6 = (pred[4,128]{1,0:T(4,128)(4,1)}, pred[4,128]{1,0:T(4,128)(4,1)S(1)}, u32[]{:S(2)}) copy-start(pred[4,128]{1,0:T(4,128)(4,1)S(1)} %broadcast_compare_fusion) | copy-start | bytes 1540
  40.9 132.9 %all-gather.10.cloned.1.call-start = ((), (), s32[]{:S(2)}) async-start(), calls=%async_computation.1 | async-start | bytes 2162688 | tf_op jit(solution)/shard_map/all_gather | solution.py:186
  90.3 2.6 copy-start.7
  92.0 35.9 %copy-start.5 = (f32[4,8,8]{2,1,0:T(8,128)S(1)}, f32[4,8,8]{2,1,0:T(8,128)}, u32[]{:S(2)}) copy-start(f32[4,8,8]{2,1,0:T(8,128)} %get-tuple-element.216) | copy-start | bytes 3076
  92.9 36.8 %copy-start.4 = (bf16[32,1024]{1,0:T(8,128)(2,1)S(1)}, bf16[32,1024]{1,0:T(8,128)(2,1)}, u32[]{:S(2)}) copy-start(bf16[32,1024]{1,0:T(8,128)(2,1)} %param.17) | copy-start | bytes 196612
  127.8 47.8 %copy-start.2 = (bf16[4,4,1024]{2,1,0:T(4,128)(2,1)S(1)}, bf16[4,4,1024]{2,1,0:T(4,128)(2,1)}, u32[]{:S(2)}) copy-start(bf16[4,4,1024]{2,1,0:T(4,128)(2,1)} %param.12) | copy-start | bytes 98308
  173.8 2.5 copy-start.1
Sparse Core Ops, SparseCore 0:
  41.1 45.7 all-gather.7
  130.7 43.0 all-gather.9
